TPU v7x, 512 devices: a whole 4x4x16 slice. The times are simulated.
512 devices in a mesh: ctx: 8 (over x_hi, y), fsdp: 64 (over x_lo, z, core).
Axes of the slice: x: 4 (x_hi: 2, x_lo: 2; x = x_hi * 2 + x_lo), y: 4, z: 16, core: 2. Of those that a mesh axis runs over, the one named last changes fastest.
Arguments:
- hidden_rows: bfloat16 [64, 1024, 4608], P('fsdp', 'ctx'), may hold values from -6 to 6
- query_proj: bfloat16 [64, 1024, 2048], P('fsdp', 'ctx'), may hold values from -10 to 10
- key_proj: bfloat16 [64, 1024, 1024], P('fsdp', 'ctx'), may hold values from -10 to 10
- value_proj: bfloat16 [64, 1024, 1024], P('fsdp', 'ctx'), may hold values from -6 to 6
- order_pos: int32 [64, 1024], P('fsdp', 'ctx'), may hold values from 0 to 1023, each once within a row
- post_gain: float32 [4608], replicated, may hold values from 0.5 to 1.5
- out_weight: bfloat16 [2048, 4608], P('fsdp', 'ctx'), may hold values from -0.125 to 0.125
Outputs:
- residual_out: bfloat16 [64, 1024, 4608], P('fsdp', 'ctx')
Inputs may be any that keep to these rules, and one draw needn't show every extreme that they name: Each document's row of order_pos holds every position of 0 to 1023 exactly once.
All inputs are finite; a program needn't handle non-finite values.
Results may differ from a plain program's by a relative error of at most 0.0053.
Values may be sent and summed in bfloat16 or wider, within the bound.
A program may use at most 64 MiB of HBM per device.

v0:
```python
import jax
import jax.numpy as jnp
from jax import lax
from jax.sharding import PartitionSpec as P

HQ = 16
HK = 8
DH = 128


score_scale = 1.0 / 12.0
soft_cap = 50.0
norm_eps = 1e-06


def weigh_keys(query_heads, query_pos, key_heads, value_heads, key_pos):
    scores = (
        jnp.einsum("thgd,nhd->hgtn", query_heads, key_heads, preferred_element_type=jnp.float32)
        * score_scale
    )
    capped = soft_cap * jnp.tanh(scores / soft_cap)
    visible = key_pos[None, :] <= query_pos[:, None]
    weights = jnp.where(visible, jnp.exp(capped), 0.0)
    rounded = weights.astype(jnp.bfloat16)
    numerator = jnp.einsum(
        "hgtn,nhd->thgd", rounded, value_heads, preferred_element_type=jnp.float32
    )
    denominator = jnp.transpose(jnp.sum(weights, axis=-1), (2, 0, 1))
    return (numerator, denominator)


def shards(hidden_rows, query_proj, key_proj, value_proj, order_pos, post_gain, out_weight):
    tokens = query_proj.shape[1]
    groups = HQ // HK
    all_positions = lax.all_gather(order_pos, "ctx", axis=1, tiled=True)[0]
    weight_block = lax.all_gather(out_weight, "fsdp", axis=0, tiled=True)
    own_pos = order_pos[0]
    query_heads = query_proj[0].reshape(tokens, HK, groups, DH)
    key_piece = lax.all_gather(key_proj, "ctx", axis=1, tiled=True)
    value_piece = lax.all_gather(value_proj, "ctx", axis=1, tiled=True)
    piece_rows = key_piece.shape[1]
    numerator, denominator = weigh_keys(
        query_heads,
        own_pos,
        key_piece[0].reshape(piece_rows, HK, DH),
        value_piece[0].reshape(piece_rows, HK, DH),
        all_positions,
    )
    numerator, denominator = (numerator, denominator)
    attended = (numerator / denominator[..., None]).astype(jnp.bfloat16).reshape(1, tokens, HQ * DH)
    projected = jnp.dot(
        lax.all_gather(attended, "ctx", axis=1, tiled=True)[0],
        weight_block,
        preferred_element_type=jnp.float32,
    )
    token_rows = lax.all_to_all(
        projected.astype(jnp.bfloat16), "ctx", split_axis=0, concat_axis=1, tiled=True
    )
    widened = token_rows.astype(jnp.float32)
    normed = (
        widened
        * lax.rsqrt(jnp.mean(widened * widened, axis=-1, keepdims=True) + norm_eps)
        * post_gain
    )
    return (hidden_rows[0].astype(jnp.float32) + normed).astype(jnp.bfloat16)[None]


def solution(mesh):
    placed = (
        P("fsdp", "ctx", None),
        P("fsdp", "ctx", None),
        P("fsdp", "ctx", None),
        P("fsdp", "ctx", None),
        P("fsdp", "ctx"),
        P(),
        P("fsdp", "ctx"),
    )
    return jax.shard_map(
        shards, mesh=mesh, in_specs=placed, out_specs=P("fsdp", "ctx", None), check_vma=False
    )
```

profile of v0, /device:TPU:1, one launch (start us, length us, event | category | flops | bytes accessed | tf_op | source)
XLA Modules:
  0.0 403.8 jit_solution(9914539973454579862)
XLA Ops:
  6.5 0.0 all-gather.7.cloned.1.call-start
  6.5 0.7 all-gather.7.cloned.1.call-update
  7.3 0.0 all-gather.5.cloned.1.call-start
  7.3 1.8 copy.13
  9.1 0.0 all-gather.5.cloned.1.call-update
  9.1 0.0 all-gather.11.cloned.1.call-start
  9.2 0.7 all-gather.11.cloned.1.call-update
  9.9 0.0 all-gather.9.cloned.1.call-start
  9.9 1.4 reshape_squeeze.10
  11.3 20.7 %all_gather.15 = s32[1,1024]{1,0:T(1,128)S(1)} all-gather(s32[1,128]{1,0:T(1,128)} %param.11), channel_id=1, replica_groups=mesh['ctx'=8,'fsdp'=64] {'ctx'}, dimensions={1}, use_global_device_ids=true | all-gather | bytes 4608 | tf_op jit(solution)/shard_map/all_gather | solution.py:35
  32.0 0.9 broadcast_compare_fusion
  32.9 52.0 %all-gather.7.cloned.1.call-done = bf16[1,1024,1024]{2,1,0:T(8,128)(2,1)} async-done(((bf16[1,128,1024]{2,1,0:T(8,128)(2,1)}), bf16[1,1024,1024]{2,1,0:T(8,128)(2,1)}) %all-gather.7.cloned.1.call-update) | async-done | bytes 2097168 | tf_op jit(solution)/shard_map/all_gather | solution.py:40
  84.8 2.9 copy.16
  87.7 68.0 %all-gather.5.cloned.1.call-done = bf16[1,1024,1024]{1,2,0:T(8,128)(2,1)} async-done(((bf16[1,128,1024]{1,2,0:T(8,128)(2,1)}), bf16[1,1024,1024]{1,2,0:T(8,128)(2,1)}) %all-gather.5.cloned.1.call-update) | async-done | bytes 2097168 | tf_op jit(solution)/shard_map/all_gather | solution.py:39
  155.6 4.1 %fusion = (f32[8,2,128]{2,1,0:T(2,128)S(1)}, f32[8,1024,128,2]{2,1,3,0:T(8,128)S(1)}) fusion(pred[128,1024]{0,1:T(8,128)(4,1)S(1)} %broadcast_compare_fusion, bf16[1024,8,128,1]{0,2,3,1:T(8,128)(2,1)} %bitcast.60, bf16[128,8,2,128]{3,2,1,0:T(2,128)(2,1)S(1)} %reshape_squeeze.10), kind=kOutput, calls=%fused_computation.1 | convolution fusion | flops 545257472 | bytes 11149312 | tf_op jit(solution)/shard_map/thgd,nhd->hgtn/dot_general | solution.py:18
  159.8 3.4 divide_convert_fusion
  163.2 0.0 all-gather.9.cloned.1.call-update
  163.2 116.4 %all-gather.11.cloned.1.call-done = bf16[2048,576]{1,0:T(8,128)(2,1)} async-done(((bf16[32,576]{1,0:T(8,128)(2,1)}), bf16[2048,576]{1,0:T(8,128)(2,1)}) %all-gather.11.cloned.1.call-update) | async-done | bytes 2359312 | tf_op jit(solution)/shard_map/all_gather | solution.py:36
  279.6 87.6 %all-gather.9.cloned.1.call-done = bf16[1,1024,2048]{1,2,0:T(8,128)(2,1)} async-done(((bf16[1,128,2048]{1,2,0:T(8,128)(2,1)}), bf16[1,1024,2048]{1,2,0:T(8,128)(2,1)}) %all-gather.9.cloned.1.call-update) | async-done | bytes 4194320 | tf_op jit(solution)/shard_map/all_gather | solution.py:52
  367.2 5.7 %fusion.13 = bf16[72,8,8,128]{3,2,1,0:T(8,128)(2,1)S(1)} fusion(bf16[2048,576]{1,0:T(8,128)(2,1)} %all-gather.11.cloned.1.call-done, bf16[1,1024,2048]{1,2,0:T(8,128)(2,1)} %all-gather.9.cloned.1.call-done), kind=kOutput, calls=%fused_computation.13 | convolution fusion | flops 2416508928 | bytes 7733248 | tf_op jit(solution)/shard_map/dot_general | solution.py:51
  372.9 0.0 copy-start
  372.9 1.2 copy.31
  374.1 3.6 all-to-all-start
  377.7 0.0 copy-done
  377.7 0.7 copy.12
  378.4 0.0 copy-start.1
  378.5 14.6 %all-to-all-done = bf16[8,128,576]{1,2,0:T(8,128)(2,1)S(1)} async-done(((bf16[8,128,576]{1,2,0:T(8,128)(2,1)}), bf16[8,128,576]{1,2,0:T(8,128)(2,1)S(1)}, u32[]{:S(2)}, u32[]{:S(2)}) %all-to-all-start) | async-done | bytes 1179680 | tf_op jit(solution)/shard_map/all_to_all | solution.py:56
  393.1 0.6 multiply_reduce_fusion
  393.7 0.2 convert_element_type.47
  393.9 0.0 copy-done.1
  393.9 2.0 fusion.9
  395.9 1.4 copy.19
  (1 shorter events, 0.0 us)
Async XLA Ops:
  6.5 78.3 %all-gather.7.cloned.1.call-start = ((), (), s32[]{:S(2)}) async-start(), calls=%async_computation.2 | async-start | bytes 2359296 | tf_op jit(solution)/shard_map/all_gather | solution.py:40
  7.3 148.4 %all-gather.5.cloned.1.call-start = ((), (), s32[]{:S(2)}) async-start(), calls=%async_computation.1 | async-start | bytes 2359296 | tf_op jit(solution)/shard_map/all_gather | solution.py:39
  9.1 270.5 %all-gather.11.cloned.1.call-start = ((), (), s32[]{:S(2)}) async-start(), calls=%async_computation.4 | async-start | bytes 2662400 | tf_op jit(solution)/shard_map/all_gather | solution.py:36
  9.9 357.4 %all-gather.9.cloned.1.call-start = ((), (), s32[]{:S(2)}) async-start(), calls=%async_computation.3 | async-start | bytes 4718592 | tf_op jit(solution)/shard_map/all_gather | solution.py:52
  372.9 4.8 %copy-start = (bf16[1,128,4608]{2,1,0:T(8,128)(2,1)S(1)}, bf16[1,128,4608]{2,1,0:T(8,128)(2,1)}, u32[]{:S(2)}) copy-start(bf16[1,128,4608]{2,1,0:T(8,128)(2,1)} %param.7) | copy-start | bytes 3538948
  374.1 18.9 %all-to-all-start = ((bf16[8,128,576]{1,2,0:T(8,128)(2,1)}), bf16[8,128,576]{1,2,0:T(8,128)(2,1)S(1)}, u32[]{:S(2)}, u32[]{:S(2)}) async-start(bf16[8,128,576]{1,2,0:T(8,128)(2,1)} %bitcast.53), calls=%async_computation | async-start | bytes 2359296 | tf_op jit(solution)/shard_map/all_to_all | solution.py:56
  378.4 15.4 %copy-start.1 = (f32[4608]{0:T(1024)S(1)}, f32[4608]{0:T(1024)}, u32[]{:S(2)}) copy-start(f32[4608]{0:T(1024)} %param.12) | copy-start | bytes 55300
Sparse Core Ops, SparseCore 0:
  10.6 74.1 all-gather.6
  87.9 67.7 all-gather.4
  157.8 121.7 all-gather.10
  282.5 84.6 all-gather.8
where the time goes:
time: 405 us; the launch traced here: 404 us
  waiting for transfers between devices  340 us (84%)
  blocking collectives  20.7 us (5%)
  matrix products  13.2 us (3%)
  between operations  13.2 us (3%)
  local copies, waits for them, and re-layouts  9.43 us (2%)
    all_gather x1, waiting for transfers between devices, shards(): weight_block = lax.all_gather(out_weight, 'fsdp', axis=0, tiled=True)  116 us
    all_gather x1, waiting for transfers between devices, shards(): lax.all_gather(attended, 'ctx', axis=1, tiled=True)[0]  87.6 us
    all_gather x1, waiting for transfers between devices, shards(): key_piece = lax.all_gather(key_proj, 'ctx', axis=1, tiled=True)  68 us
    all_gather x1, waiting for transfers between devices, shards(): value_piece = lax.all_gather(value_proj, 'ctx', axis=1, tiled=True)  52 us
    all_gather x1, blocking collectives, shards(): all_positions = lax.all_gather(order_pos, 'ctx', axis=1, tiled=True)[0]  20.7 us
    all_to_all x1, waiting for transfers between devices, shards(): lax.all_to_all(projected.astype(jnp.bfloat16), 'ctx', split_axis=0, conca...  14.6 us
  transfers between devices with their start and end apart: 5, of which 5 were waited for; matrix products, arithmetic and copies ran while one was open for 4% of the time, Pallas kernels for 0%

commit v1 on v0

v1 whole, which is shorter than its diff:
```python
import jax
import jax.numpy as jnp
from jax import lax
from jax.experimental import pallas as pl
from jax.experimental.pallas import tpu as pltpu
from jax.sharding import PartitionSpec as P

D = 4608
TB = 128
CB = 576
NZ = 16
INNER = 1.0 / 600.0
OUTER = 50.0 * 1.4426950408889634
NORM_EPS = 1e-06
MESH = pl.DeviceIdType.MESH


def body(
    hid, q, k, v, pos, gain, w, out,
    qbuf, kbuf, vbuf, pbuf, bias, att, wg, acc, obuf, rows, hbuf,
    loc, q_s, q_r, k_s, k_r, v_s, v_r, p_s, p_r, wx_s, wx_r,
    rg_s, rg_r, sb_s, sb_r, a_s, a_r, f_s, f_r, o_s, o_r,
):
    ctx = lax.axis_index("ctx")
    fs = lax.axis_index("fsdp")
    xh, y = ctx // 4, ctx % 4
    xl, z, core = fs // 32, (fs // 2) % NZ, fs % 2
    step_z = 1 - 2 * core
    sends = []

    def dev_y(d):
        return (xh * 4 + (y + d) % 4, fs)

    def dev_ctx(flip, d):
        return (((xh + flip) % 2) * 4 + (y + d) % 4, fs)

    def dev_x(fh, fl):
        return (((xh + fh) % 2) * 4 + y, ((xl + fl) % 2) * 32 + fs % 32)

    x_opp = dev_ctx(1, 0)
    z_next = (ctx, xl * 32 + ((z + step_z + NZ) % NZ) * 2 + core)
    z_prev = (ctx, xl * 32 + ((z - step_z + NZ) % NZ) * 2 + core)
    sibling = (ctx, fs + step_z)

    def remote(src, dst, ss, rs, dev):
        return pltpu.make_async_remote_copy(
            src_ref=src, dst_ref=dst, send_sem=ss, recv_sem=rs, device_id=dev, device_id_type=MESH
        )

    def send(src, dst, ss, rs, dev):
        c = remote(src, dst, ss, rs, dev)
        c.start()
        sends.append(c)

    partners = [dev_ctx(f, d) for f in range(2) for d in range(4) if f or d]
    partners += [dev_x(0, 1), dev_x(1, 1), z_next, z_prev, sibling]
    barrier = pltpu.get_barrier_semaphore()
    for dev in partners:
        pl.semaphore_signal(barrier, inc=1, device_id=dev, device_id_type=MESH)

    wrow = pl.multiple_of(core * 32, 32)
    kcol = pl.multiple_of(y * 256, 256)
    qcol = pl.multiple_of(y * 512, 512)
    own = [
        pltpu.make_async_copy(w, wg.at[xh, xl, z, pl.ds(wrow, 32)], loc.at[0]),
        pltpu.make_async_copy(k.at[0, :, pl.ds(kcol, 256)], kbuf.at[ctx], loc.at[1]),
        pltpu.make_async_copy(v.at[0, :, pl.ds(kcol, 256)], vbuf.at[ctx], loc.at[2]),
        pltpu.make_async_copy(q.at[0, :, pl.ds(qcol, 512)], qbuf.at[y], loc.at[3]),
        pltpu.make_async_copy(pos, pbuf.at[ctx], loc.at[4]),
        pltpu.make_async_copy(hid.at[0], hbuf, loc.at[5]),
    ]
    for c in own:
        c.start()
    pl.semaphore_wait(barrier, len(partners))

    for i, (fh, fl) in enumerate(((0, 1), (1, 0), (1, 1))):
        send(w, wg.at[xh, xl, z, pl.ds(wrow, 32)], wx_s.at[i], wx_r.at[i], dev_x(fh, fl))
    for f in range(2):
        for d in range(4):
            if f or d:
                i = f * 4 + d
                send(pos, pbuf.at[ctx], p_s.at[i], p_r.at[i], dev_ctx(f, d))
    for d in (1, 3, 2):
        col = pl.multiple_of(((y + d) % 4) * 256, 256)
        send(k.at[0, :, pl.ds(col, 256)], kbuf.at[ctx], k_s.at[d], k_r.at[d], dev_y(d))
        send(v.at[0, :, pl.ds(col, 256)], vbuf.at[ctx], v_s.at[d], v_r.at[d], dev_y(d))
    send(k.at[0, :, pl.ds(kcol, 256)], kbuf.at[ctx], k_s.at[4], k_r.at[4], x_opp)
    send(v.at[0, :, pl.ds(kcol, 256)], vbuf.at[ctx], v_s.at[4], v_r.at[4], x_opp)
    for d in (1, 3, 2):
        col = pl.multiple_of(((y + d) % 4) * 512, 512)
        send(q.at[0, :, pl.ds(col, 512)], qbuf.at[y], q_s.at[d], q_r.at[d], dev_y(d))

    def arrived(dst, sem):
        remote(dst, dst, loc.at[6], sem, sibling).wait_recv()

    for i, (fh, fl) in enumerate(((0, 1), (1, 0), (1, 1))):
        arrived(wg.at[(xh + fh) % 2, (xl + fl) % 2, z, pl.ds(wrow, 32)], wx_r.at[i])
    own[0].wait()
    mine = wg.at[:, :, z, pl.ds(wrow, 32)]
    send(mine, mine, sb_s.at[8, 0], sb_r.at[8, 0], sibling)
    orow = pl.multiple_of((1 - core) * 32, 32)
    arrived(wg.at[:, :, z, pl.ds(orow, 32)], sb_r.at[8, 0])
    for h in range(2):
        send(wg.at[h, :, z], wg.at[h, :, z], rg_s.at[0, h], rg_r.at[0, h], z_next)

    for d in (1, 3, 2):
        src = xh * 4 + (y - d + 4) % 4
        arrived(kbuf.at[src], k_r.at[d])
        send(kbuf.at[src], kbuf.at[src], k_s.at[4 + d], k_r.at[4 + d], x_opp)
        arrived(vbuf.at[src], v_r.at[d])
        send(vbuf.at[src], vbuf.at[src], v_s.at[4 + d], v_r.at[4 + d], x_opp)

    def ring_step(s):
        zb = (z - step_z * (s + 1) + 2 * NZ) % NZ
        for h in range(2):

            def take(h=h):
                blk = wg.at[h, :, zb]
                arrived(blk, rg_r.at[s, h])
                if s < 6:
                    send(blk, blk, rg_s.at[s + 1, h], rg_r.at[s + 1, h], z_next)
                if s == 6:

                    @pl.when(core == h)
                    def _():
                        remote(blk, blk, rg_s.at[7, 0], rg_r.at[7, 0], z_next).start()

                send(blk, blk, sb_s.at[s, h], sb_r.at[s, h], sibling)

            take()

    def ring_last():
        zb = (z + NZ // 2) % NZ
        blk = wg.at[core, :, zb]
        arrived(blk, rg_r.at[7, 0])
        send(blk, blk, sb_s.at[7, 0], sb_r.at[7, 0], sibling)

    ring_step(0)
    ring_step(1)

    for c in own[1:]:
        c.wait()
    for f in range(2):
        for d in range(4):
            if f or d:
                arrived(pbuf.at[((xh + f) % 2) * 4 + (y - d + 4) % 4], p_r.at[f * 4 + d])
    for d in range(4):
        src = (1 - xh) * 4 + (y - d + 4) % 4
        arrived(kbuf.at[src], k_r.at[4 + d])
        arrived(vbuf.at[src], v_r.at[4 + d])

    def attend(t):
        prow = pbuf[xh * 4 + t].astype(jnp.float32)
        pcol = jnp.transpose(jnp.broadcast_to(prow, (TB, TB)), (1, 0))
        for c in range(8):
            key_pos = pbuf[c].astype(jnp.float32)
            bias[:, c * TB : (c + 1) * TB] = jnp.where(key_pos <= pcol, 0.0, -1e30)

        def head(h, _):
            g = h // 2
            col = pl.multiple_of(h * 128, 128)
            gcol = pl.multiple_of(g * 128, 128)
            keys = kbuf[:, :, pl.ds(gcol, 128)].reshape(8 * TB, 128)
            vals = vbuf[:, :, pl.ds(gcol, 128)].reshape(8 * TB, 128)
            qh = qbuf[t, :, pl.ds(col, 128)]
            s = lax.dot_general(qh, keys, (((1,), (1,)), ((), ())), preferred_element_type=jnp.float32)
            p = jnp.exp2(jnp.tanh(s * INNER) * OUTER + bias[...])
            den = jnp.sum(p, axis=-1, keepdims=True)
            num = jnp.dot(p.astype(jnp.bfloat16), vals, preferred_element_type=jnp.float32)
            att[y, pl.ds(pl.multiple_of(t * TB, TB), TB), pl.ds(col, 128)] = (num / den).astype(jnp.bfloat16)
            return 0

        lax.fori_loop(0, 4, head, 0)

    def att_rows(src, lo, n):
        return att.at[src, pl.ds(pl.multiple_of(lo, 64), n)]

    def att_forward(i):
        for side, d in enumerate((1, 3)):
            src = (y - d + 4) % 4
            t = (src + i) % 4
            arrived(att_rows(src, t * TB, TB), a_r.at[side, i])
            half = att_rows(src, t * TB + side * 64, 64)
            send(half, half, f_s.at[side, i], f_r.at[side, i], dev_y(d))

    for i in range(4):
        t = (y + i) % 4
        if i > 0:
            dq = 4 - i
            arrived(qbuf.at[t], q_r.at[dq])
        attend(t)
        blk = att_rows(y, t * TB, TB)
        for side, d in enumerate((1, 3)):
            send(blk, blk, a_s.at[side, i], a_r.at[side, i], dev_y(d))
        if i > 0:
            att_forward(i - 1)
        ring_step(2 + i)
    att_forward(3)
    ring_step(6)
    ring_last()
    for s in range(7):
        zb = (z + step_z * (s + 1) + 2 * NZ) % NZ
        for h in range(2):
            arrived(wg.at[h, :, zb], sb_r.at[s, h])
    arrived(wg.at[1 - core, :, (z + NZ // 2) % NZ], sb_r.at[7, 0])

    def project(src, first):
        wl, wz = src // 2, (src % 2) * 8

        def part(i, _):
            b, m = i // 2, pl.multiple_of((i % 2) * 256, 256)
            wb = wg[b, wl, pl.ds(wz, 8)].reshape(512, CB)
            r = jnp.dot(att[src, pl.ds(m, 256)], wb, preferred_element_type=jnp.float32)
            if first:
                acc[b, pl.ds(m, 256)] = r
            else:
                acc[b, pl.ds(m, 256)] += r
            return 0

        lax.fori_loop(0, 4, part, 0)

    project(y, True)
    project((y + 3) % 4, False)
    project((y + 1) % 4, False)
    far = (y + 2) % 4
    for i in range(4):
        for side, d in enumerate((1, 3)):
            t = (far + i) % 4
            arrived(att_rows(far, t * TB + side * 64, 64), f_r.at[side, i])
    wl, wz = far // 2, (far % 2) * 8
    for b in range(2):

        def last(m, _, b=b):
            m = pl.multiple_of(m * 256, 256)
            wb = wg[b, wl, pl.ds(wz, 8)].reshape(512, CB)
            r = jnp.dot(att[far, pl.ds(m, 256)], wb, preferred_element_type=jnp.float32)
            obuf[b, pl.ds(m, 256)] = (acc[b, pl.ds(m, 256)] + r).astype(jnp.bfloat16)
            return 0

        lax.fori_loop(0, 2, last, 0)
        for d in (2, 1, 3):
            t = (y + d) % 4
            src = obuf.at[b, pl.ds(pl.multiple_of(t * TB, TB), TB)]
            send(src, rows.at[b * 4 + y], o_s.at[b, d], o_r.at[b, d], dev_y(d))
        rows[b * 4 + y] = obuf[b, pl.ds(pl.multiple_of(y * TB, TB), TB)]
    for b in range(2):
        for d in (1, 3, 2):
            arrived(rows.at[b * 4 + (y - d + 4) % 4], o_r.at[b, d])

    def norm(i, _):
        r = pl.ds(pl.multiple_of(i * 32, 32), 32)
        ss = jnp.zeros((32, 1), jnp.float32)
        for c in range(8):
            x = rows[c, r].astype(jnp.float32)
            ss += jnp.sum(x * x, axis=-1, keepdims=True)
        scale = lax.rsqrt(ss * (1.0 / D) + NORM_EPS)
        for c in range(8):
            cols = slice(c * CB, (c + 1) * CB)
            x = rows[c, r].astype(jnp.float32) * scale * gain[:, cols]
            out[0, r, cols] = (hbuf[r, cols].astype(jnp.float32) + x).astype(jnp.bfloat16)
        return 0

    lax.fori_loop(0, 4, norm, 0)

    for c in sends:
        c.wait_send()
    last_blk = wg.at[core, :, (z - step_z * 7 + 2 * NZ) % NZ]
    remote(last_blk, last_blk, rg_s.at[7, 0], rg_r.at[7, 0], z_next).wait_send()


def shards(hidden_rows, query_proj, key_proj, value_proj, order_pos, post_gain, out_weight):
    hbm = pl.BlockSpec(memory_space=pl.ANY)
    vmem = pl.BlockSpec(memory_space=pltpu.VMEM)
    bf16, f32, dma = jnp.bfloat16, jnp.float32, pltpu.SemaphoreType.DMA
    return pl.pallas_call(
        body,
        name="sublayer",
        out_shape=jax.ShapeDtypeStruct((1, TB, D), bf16),
        in_specs=[hbm, hbm, hbm, hbm, hbm, vmem, hbm],
        out_specs=vmem,
        scratch_shapes=[
            pltpu.VMEM((4, TB, 512), bf16),
            pltpu.VMEM((8, TB, 256), bf16),
            pltpu.VMEM((8, TB, 256), bf16),
            pltpu.VMEM((8, 1, TB), jnp.int32),
            pltpu.VMEM((TB, 8 * TB), f32),
            pltpu.VMEM((4, 512, 512), bf16),
            pltpu.VMEM((2, 2, NZ, 64, CB), bf16),
            pltpu.VMEM((2, 512, CB), f32),
            pltpu.VMEM((2, 512, CB), bf16),
            pltpu.VMEM((8, TB, CB), bf16),
            pltpu.VMEM((TB, D), bf16),
            dma((7,)),
            dma((4,)), dma((4,)),
            dma((8,)), dma((8,)),
            dma((8,)), dma((8,)),
            dma((8,)), dma((8,)),
            dma((3,)), dma((3,)),
            dma((8, 2)), dma((8, 2)),
            dma((9, 2)), dma((9, 2)),
            dma((2, 4)), dma((2, 4)),
            dma((2, 4)), dma((2, 4)),
            dma((2, 4)), dma((2, 4)),
        ],
        compiler_params=pltpu.CompilerParams(
            collective_id=0, has_side_effects=True, vmem_limit_bytes=48 << 20
        ),
    )(hidden_rows, query_proj, key_proj, value_proj, order_pos, post_gain.reshape(1, D), out_weight)


def solution(mesh):
    placed = (
        P("fsdp", "ctx", None),
        P("fsdp", "ctx", None),
        P("fsdp", "ctx", None),
        P("fsdp", "ctx", None),
        P("fsdp", "ctx"),
        P(),
        P("fsdp", "ctx"),
    )
    return jax.shard_map(
        shards, mesh=mesh, in_specs=placed, out_specs=P("fsdp", "ctx", None), check_vma=False
    )
```

time: 405 us -> 91.8 us (0.23)
  waiting for transfers between devices: 340 us -> 0 us
  Pallas kernels: 0 us -> 84 us
  blocking collectives: 20.7 us -> 0 us
  matrix products: 13.2 us -> 0 us
  between operations: 13.2 us -> 0.03 us
    all_gather x4 -> x0, waiting for transfers between devices: 324 us -> none  [the longest x1 116 us: shards(): weight_block = lax.all_gather(out_weight, 'fsdp', axis=0, tiled=True)]
    pallas_call x0 -> x1, Pallas kernels: none -> 84 us  [shards(): pl.pallas_call(body, name='sublayer', out_shape=jax.ShapeDtypeStruct((1,...]
    all_gather x1 -> x0, blocking collectives: 20.7 us -> none  [shards(): all_positions = lax.all_gather(order_pos, 'ctx', axis=1, tiled=True)[0]]
    all_to_all x1 -> x0, waiting for transfers between devices: 14.6 us -> none  [shards(): lax.all_to_all(projected.astype(jnp.bfloat16), 'ctx', split_axis=0, conca...]
    dot_general x3 -> x0, matrix products: 13.2 us -> none  [the longest x1 5.67 us: shards(): jnp.dot(lax.all_gather(attended, 'ctx', axis=1, tiled=True)[0], weight_bl...]
    unnamed x6 -> x13, local copies, waits for them, and re-layouts: 2.53 us -> 6.65 us
  transfers between devices with their start and end apart: 5 -> 0, of which waited for: 5 -> 0; matrix products, arithmetic and copies ran while one was open for 4% -> 0% of each run, Pallas kernels for 0% -> 0%
where the time goes in v1:
time: 91.8 us; the launch traced here: 91.5 us
  Pallas kernels  84 us (92%)
  local copies, waits for them, and re-layouts  7.39 us (8%)
    pallas_call x1, Pallas kernels, shards(): pl.pallas_call(body, name='sublayer', out_shape=jax.ShapeDtypeStruct((1,...  84 us
    unnamed x13, local copies, waits for them, and re-layouts  6.65 us

profile of v1, /device:TPU:1, one launch (start us, length us, event | category | flops | bytes accessed | tf_op | source)
XLA Modules:
  0.0 91.5 jit_solution(14500612250164260105)
XLA Ops:
  0.0 0.7 reshape.3.gain
  0.7 0.0 copy-start
  0.8 1.3 %copy-done = bf16[1,128,4608]{2,1,0:T(8,128)(2,1)S(1)} copy-done((bf16[1,128,4608]{2,1,0:T(8,128)(2,1)S(1)}, bf16[1,128,4608]{2,1,0:T(8,128)(2,1)}, u32[]{:S(2)}) %copy-start) | copy-done | bytes 1179672
  2.0 0.0 copy-start.1
  2.0 1.0 %copy-done.1 = bf16[1,128,2048]{2,1,0:T(8,128)(2,1)S(1)} copy-done((bf16[1,128,2048]{2,1,0:T(8,128)(2,1)S(1)}, bf16[1,128,2048]{2,1,0:T(8,128)(2,1)}, u32[]{:S(2)}) %copy-start.1) | copy-done | bytes 524312
  3.1 0.0 copy-start.2
  3.1 0.9 %copy-done.2 = bf16[1,128,1024]{2,1,0:T(8,128)(2,1)S(1)} copy-done((bf16[1,128,1024]{2,1,0:T(8,128)(2,1)S(1)}, bf16[1,128,1024]{2,1,0:T(8,128)(2,1)}, u32[]{:S(2)}) %copy-start.2) | copy-done | bytes 262168
  4.0 0.0 copy-start.3
  4.0 0.9 %copy-done.3 = bf16[1,128,1024]{2,1,0:T(8,128)(2,1)S(1)} copy-done((bf16[1,128,1024]{2,1,0:T(8,128)(2,1)S(1)}, bf16[1,128,1024]{2,1,0:T(8,128)(2,1)}, u32[]{:S(2)}) %copy-start.3) | copy-done | bytes 262168
  5.0 0.0 copy-start.4
  5.0 0.8 copy-done.4
  5.7 0.0 copy-start.5
  5.7 0.7 copy-done.5
  6.4 84.0 %sublayer.1 = bf16[1,128,4608]{2,1,0:T(8,128)(2,1)S(1)} custom-call(bf16[1,128,4608]{2,1,0:T(8,128)(2,1)S(1)} %copy-done, bf16[1,128,2048]{2,1,0:T(8,128)(2,1)S(1)} %copy-done.1, bf16[1,128,1024]{2,1,0:T(8,128)(2,1)S(1)} %copy-done.2, bf16[1,128,1024]{2,1,0:T(8,128)(2,1)S(1)} %copy-done.3, s32[1,128]{1,0:T(1,128)S(1)} %copy-done.5, ...), custom_call_target="tpu_custom_call" | custom-call | tf_op jit(solution)/shard_map/sublayer/pallas_call | solution.py:275
  90.4 1.0 %copy.9 = bf16[1,128,4608]{2,1,0:T(8,128)(2,1)} copy(bf16[1,128,4608]{2,1,0:T(8,128)(2,1)S(1)} %sublayer.1) | data formatting | bytes 2359296
Async XLA Ops:
  0.7 1.3 %copy-start = (bf16[1,128,4608]{2,1,0:T(8,128)(2,1)S(1)}, bf16[1,128,4608]{2,1,0:T(8,128)(2,1)}, u32[]{:S(2)}) copy-start(bf16[1,128,4608]{2,1,0:T(8,128)(2,1)} %hid.1) | copy-start | bytes 3538948
  2.0 1.0 %copy-start.1 = (bf16[1,128,2048]{2,1,0:T(8,128)(2,1)S(1)}, bf16[1,128,2048]{2,1,0:T(8,128)(2,1)}, u32[]{:S(2)}) copy-start(bf16[1,128,2048]{2,1,0:T(8,128)(2,1)} %q.1) | copy-start | bytes 1572868
  3.1 0.9 %copy-start.2 = (bf16[1,128,1024]{2,1,0:T(8,128)(2,1)S(1)}, bf16[1,128,1024]{2,1,0:T(8,128)(2,1)}, u32[]{:S(2)}) copy-start(bf16[1,128,1024]{2,1,0:T(8,128)(2,1)} %k.1) | copy-start | bytes 786436
  4.0 0.9 %copy-start.3 = (bf16[1,128,1024]{2,1,0:T(8,128)(2,1)S(1)}, bf16[1,128,1024]{2,1,0:T(8,128)(2,1)}, u32[]{:S(2)}) copy-start(bf16[1,128,1024]{2,1,0:T(8,128)(2,1)} %v.1) | copy-start | bytes 786436
  5.0 0.8 copy-start.4
  5.7 0.7 copy-start.5

commit v2 on v0

v2 whole, which is shorter than its diff:
```python
import jax
import jax.numpy as jnp
from jax import lax
from jax.experimental import pallas as pl
from jax.experimental.pallas import tpu as pltpu
from jax.sharding import PartitionSpec as P

D = 4608
OTHERS = [(0, 1), (1, 0), (1, 1)]
TB = 128
HB = 64
CB = 576
CP = 2 * CB
NZ = 16
INNER = 1.0 / 600.0
OUTER = 50.0 * 1.4426950408889634
NORM_EPS = 1e-06
MESH = pl.DeviceIdType.MESH
AWAY = [0, 1, -1, 2, -2, 3, -3, 4, -4, 5, -5, 6, -6, 7, -7, 8]


def body(
    hid, q, k, v, pos, gain, w, out,
    qbuf, kbuf, vbuf, pbuf, bias, att, wst, wf, wg, obuf, rows, hbuf, gbuf, res,
    loc, q_s, q_r, k_s, k_r, v_s, v_r, p_s, p_r, wz_s, wz_r, wx_s, wx_r,
    sb_s, sb_r, a_s, a_r, f_s, f_r, o_s, o_r,
):
    ctx = lax.axis_index("ctx")
    fs = lax.axis_index("fsdp")
    xh, y = ctx // 4, ctx % 4
    xl, z, core = fs // 32, (fs // 2) % NZ, fs % 2
    sends = []

    def dev_y(d):
        return (xh * 4 + (y + d) % 4, fs)

    def dev_ctx(flip, d):
        return (((xh + flip) % 2) * 4 + (y + d) % 4, fs)

    def dev_x(fh, fl):
        return (((xh + fh) % 2) * 4 + y, ((xl + fl) % 2) * 32 + fs % 32)

    x_opp = dev_ctx(1, 0)
    sibling = (ctx, fs + 1 - 2 * core)

    def dev_z(d):
        return (ctx, xl * 32 + ((z + d + NZ) % NZ) * 2 + core)

    def remote(src, dst, ss, rs, dev):
        return pltpu.make_async_remote_copy(
            src_ref=src, dst_ref=dst, send_sem=ss, recv_sem=rs, device_id=dev, device_id_type=MESH
        )

    def send(src, dst, ss, rs, dev):
        c = remote(src, dst, ss, rs, dev)
        c.start()
        sends.append(c)

    def arrived(dst, sem):
        remote(dst, dst, loc.at[6], sem, sibling).wait_recv()

    partners = [dev_ctx(f, d) for f in range(2) for d in range(4) if f or d]
    partners += [dev_x(0, 1), dev_x(1, 1), sibling] + [dev_z(d) for d in AWAY[1:]]
    barrier = pltpu.get_barrier_semaphore()
    for dev in partners:
        pl.semaphore_signal(barrier, inc=1, device_id=dev, device_id_type=MESH)

    kcol = pl.multiple_of(y * 256, 256)
    qcol = pl.multiple_of(y * 512, 512)
    own = [
        pltpu.make_async_copy(w, wst, loc.at[0]),
        pltpu.make_async_copy(k.at[0, :, pl.ds(kcol, 256)], kbuf.at[ctx], loc.at[1]),
        pltpu.make_async_copy(v.at[0, :, pl.ds(kcol, 256)], vbuf.at[ctx], loc.at[2]),
        pltpu.make_async_copy(q.at[0, :, pl.ds(qcol, 512)], qbuf.at[y], loc.at[3]),
        pltpu.make_async_copy(pos, pbuf.at[ctx], loc.at[4]),
        pltpu.make_async_copy(hid.at[0], hbuf, loc.at[5]),
        pltpu.make_async_copy(gain, gbuf.at[0], loc.at[7]),
    ]
    for c in own:
        c.start()
    own[0].wait()
    wf[xh, xl, core, 0] = jnp.concatenate([wst[0:16], wst[16:32]], axis=1)
    pl.semaphore_wait(barrier, len(partners))

    for d in (1, 3, 2):
        col = pl.multiple_of(((y + d) % 4) * 256, 256)
        send(k.at[0, :, pl.ds(col, 256)], kbuf.at[ctx], k_s.at[d], k_r.at[d], dev_y(d))
        send(v.at[0, :, pl.ds(col, 256)], vbuf.at[ctx], v_s.at[d], v_r.at[d], dev_y(d))
    send(k.at[0, :, pl.ds(kcol, 256)], kbuf.at[ctx], k_s.at[4], k_r.at[4], x_opp)
    send(v.at[0, :, pl.ds(kcol, 256)], vbuf.at[ctx], v_s.at[4], v_r.at[4], x_opp)
    for f in range(2):
        for d in range(4):
            if f or d:
                i = f * 4 + d
                send(pos, pbuf.at[ctx], p_s.at[i], p_r.at[i], dev_ctx(f, d))

    own_w = wf.at[xh, xl, core, 0]
    for r, d in enumerate(AWAY):
        if r:
            back = AWAY.index(-d if d < 8 else 8)
            send(own_w, wf.at[xh, xl, core, back], wz_s.at[r], wz_r.at[back], dev_z(d))
    for d in (1, 3, 2):
        col = pl.multiple_of(((y + d) % 4) * 512, 512)
        send(q.at[0, :, pl.ds(col, 512)], qbuf.at[y], q_s.at[d], q_r.at[d], dev_y(d))

    def forward_kv(d):
        src = xh * 4 + (y - d + 4) % 4
        arrived(kbuf.at[src], k_r.at[d])
        send(kbuf.at[src], kbuf.at[src], k_s.at[4 + d], k_r.at[4 + d], x_opp)
        arrived(vbuf.at[src], v_r.at[d])
        send(vbuf.at[src], vbuf.at[src], v_s.at[4 + d], v_r.at[4 + d], x_opp)

    forward_kv(1)
    forward_kv(3)
    forward_kv(2)

    def batch(ref_h, ref_l, c, b):
        return wf.at[ref_h, ref_l, c, pl.ds(4 * b, 4)]

    def weights_z(b):
        for r in range(max(4 * b, 1), 4 * b + 4):
            arrived(wf.at[xh, xl, core, r], wz_r.at[r])
        src = batch(xh, xl, core, b)
        for i, (fh, fl) in enumerate(OTHERS):
            send(src, src, wx_s.at[i, b], wx_r.at[i, b], dev_x(fh, fl))
        send(src, src, sb_s.at[3, b], sb_r.at[3, b], sibling)

    def weights_x(b):
        for i, (fh, fl) in enumerate(OTHERS):
            src = batch((xh + fh) % 2, (xl + fl) % 2, core, b)
            arrived(src, wx_r.at[i, b])
            send(src, src, sb_s.at[i, b], sb_r.at[i, b], sibling)

    def unfold(b):
        for i, (fh, fl) in enumerate(OTHERS + [(0, 0)]):
            arrived(batch((xh + fh) % 2, (xl + fl) % 2, 1 - core, b), sb_r.at[i, b])

        def piece(i, _):
            l, c = i // 2, i % 2
            for r in range(4 * b, 4 * b + 4):
                zb = (z + AWAY[r] + NZ) % NZ
                lo, hi = wf[0, l, c, r], wf[1, l, c, r]
                top = pl.multiple_of(c * 32, 32)
                wg[l, zb, pl.ds(top, 16)] = jnp.concatenate([lo[:, :CB], hi[:, :CB]], axis=1)
                wg[l, zb, pl.ds(top + 16, 16)] = jnp.concatenate([lo[:, CB:], hi[:, CB:]], axis=1)
            return 0

        lax.fori_loop(0, 4, piece, 0)

    for f in range(2):
        for d in range(4):
            if f or d:
                arrived(pbuf.at[((xh + f) % 2) * 4 + (y - d + 4) % 4], p_r.at[f * 4 + d])
    own[4].wait()
    for t in range(4):
        prow = pbuf[xh * 4 + t].astype(jnp.float32)
        pcol = jnp.transpose(jnp.broadcast_to(prow, (TB, TB)), (1, 0))
        for c in range(8):
            seen = jnp.where(pbuf[c].astype(jnp.float32) <= pcol, 0.0, -1e30)
            for p in range(2):
                bias[p, t * HB : (t + 1) * HB, c * TB : (c + 1) * TB] = seen[p * HB : (p + 1) * HB]

    weights_z(0)
    for c in own[1:4] + own[5:]:
        c.wait()
    for d in (1, 3, 2):
        arrived(qbuf.at[(y - d + 4) % 4], q_r.at[d])
    weights_z(1)
    for d in range(4):
        src = (1 - xh) * 4 + (y - d + 4) % 4
        arrived(kbuf.at[src], k_r.at[4 + d])
        arrived(vbuf.at[src], v_r.at[4 + d])

    def attend(p, h):
        gcol = pl.multiple_of((h // 2) * 128, 128)
        qh = qbuf[:, pl.ds(pl.multiple_of(p * HB, HB), HB), pl.ds(pl.multiple_of(h * 128, 128), 128)]
        qh = qh.reshape(4 * HB, 128)
        num = den = 0.0
        for c in range(4):
            keys = kbuf[2 * c : 2 * c + 2, :, pl.ds(gcol, 128)].reshape(2 * TB, 128)
            vals = vbuf[2 * c : 2 * c + 2, :, pl.ds(gcol, 128)].reshape(2 * TB, 128)
            s = lax.dot_general(qh, keys, (((1,), (1,)), ((), ())), preferred_element_type=jnp.float32)
            e = jnp.exp2(jnp.tanh(s * INNER) * OUTER + bias[p, :, c * 256 : (c + 1) * 256])
            den += e[:, :128] + e[:, 128:]
            num += jnp.dot(e.astype(jnp.bfloat16), vals, preferred_element_type=jnp.float32)
        den = jnp.sum(den, axis=-1, keepdims=True)
        att[y, p, h] = (num / den).astype(jnp.bfloat16)

    def att_forward(u):
        p, h = u // 4, u % 4
        for side, d in enumerate((1, 3)):
            src = (y - d + 4) % 4
            arrived(att.at[src, p, h], a_r.at[side, u])
            half = att.at[src, p, h, pl.ds(side * TB, TB)]
            remote(half, half, f_s.at[side, u], f_r.at[side, u], dev_y(d)).start()

    def unit(u, _):
        p, h = u // 4, u % 4
        attend(p, h)
        blk = att.at[y, p, h]
        for side, d in enumerate((1, 3)):
            remote(blk, blk, a_s.at[side, u], a_r.at[side, u], dev_y(d)).start()

        @pl.when(u >= 4)
        def _():
            att_forward(u - 4)

        return 0

    lax.fori_loop(0, 4, unit, 0)
    weights_z(2)
    weights_x(0)
    lax.fori_loop(4, 8, unit, 0)
    weights_z(3)
    weights_x(1)
    unfold(0)
    att_forward(4)
    att_forward(5)

    far = (y + 2) % 4

    def far_arrived(p):
        for h in range(4):
            for side in range(2):
                arrived(att.at[far, p, h, pl.ds(side * TB, TB)], f_r.at[side, p * 4 + h])

    def project(p):
        def cols(n, _):
            n = pl.multiple_of(n * 384, 384)
            r = 0.0
            for src in range(4):
                a = jnp.concatenate([att[src, p, h] for h in range(4)], axis=1)
                wb = wg[src // 2, (src % 2) * 8 : (src % 2) * 8 + 8, :, pl.ds(n, 384)].reshape(512, 384)
                r += jnp.dot(a, wb, preferred_element_type=jnp.float32)
            obuf[p, :, :, pl.ds(n, 384)] = r.astype(jnp.bfloat16).reshape(4, HB, 384)
            return 0

        lax.fori_loop(0, 3, cols, 0)
        for d in (2, 1, 3):
            dst = rows.at[p, y]
            send(obuf.at[p, (y + d) % 4], dst, o_s.at[p, d], o_r.at[p, d], dev_y(d))
        rows[p, y] = obuf[p, y]

    def norm(p):
        for d in (1, 3, 2):
            arrived(rows.at[p, (y - d + 4) % 4], o_r.at[p, d])

        def piece(i, _):
            r = pl.ds(pl.multiple_of(i * 32, 32), 32)
            t = pl.ds(pl.multiple_of(p * HB + i * 32, 32), 32)
            ss = jnp.zeros((32, 1), jnp.float32)
            for c in range(4):
                x = rows[p, c, r].astype(jnp.float32)
                ss += jnp.sum(x * x, axis=-1, keepdims=True)
            scale = lax.rsqrt(ss * (1.0 / D) + NORM_EPS)
            for c in range(4):
                x = rows[p, c, r].astype(jnp.float32) * scale
                for b in range(2):
                    cols = slice(b * 4 * CB + c * CB, b * 4 * CB + (c + 1) * CB)
                    n = x[:, b * CB : (b + 1) * CB] * gbuf[:, cols]
                    res[t, cols] = (hbuf[t, cols].astype(jnp.float32) + n).astype(jnp.bfloat16)
            return 0

        lax.fori_loop(0, 2, piece, 0)
        done = pl.ds(p * HB, HB)
        return pltpu.make_async_copy(res.at[done], out.at[0, done], loc.at[8 + p])

    weights_x(2)
    unfold(1)
    att_forward(6)
    weights_x(3)
    unfold(2)
    att_forward(7)
    far_arrived(0)
    unfold(3)
    project(0)
    far_arrived(1)
    project(1)
    first = norm(0)
    first.start()
    second = norm(1)
    second.start()
    first.wait()
    second.wait()

    for c in sends:
        c.wait_send()
    for u in range(8):
        for side in range(2):
            blk = att.at[0, 0, 0]
            remote(blk, blk, a_s.at[side, u], loc.at[6], sibling).wait_send()
            blk = att.at[0, 0, 0, pl.ds(0, TB)]
            remote(blk, blk, f_s.at[side, u], loc.at[6], sibling).wait_send()


def shards(hidden_rows, query_proj, key_proj, value_proj, order_pos, post_gain, out_weight):
    hbm = pl.BlockSpec(memory_space=pl.ANY)
    bf16, f32, dma = jnp.bfloat16, jnp.float32, pltpu.SemaphoreType.DMA
    return pl.pallas_call(
        body,
        name="sublayer",
        out_shape=jax.ShapeDtypeStruct((1, TB, D), bf16),
        in_specs=[hbm] * 7,
        out_specs=hbm,
        scratch_shapes=[
            pltpu.VMEM((4, TB, 512), bf16),
            pltpu.VMEM((8, TB, 256), bf16),
            pltpu.VMEM((8, TB, 256), bf16),
            pltpu.VMEM((8, 1, TB), jnp.int32),
            pltpu.VMEM((2, 4 * HB, 8 * TB), f32),
            pltpu.VMEM((4, 2, 4, 4 * HB, 128), bf16),
            pltpu.VMEM((32, CB), bf16),
            pltpu.VMEM((2, 2, 2, NZ, 16, CP), bf16),
            pltpu.VMEM((2, NZ, 64, CP), bf16),
            pltpu.VMEM((2, 4, HB, CP), bf16),
            pltpu.VMEM((2, 4, HB, CP), bf16),
            pltpu.VMEM((TB, D), bf16),
            pltpu.VMEM((1, D), f32),
            pltpu.VMEM((TB, D), bf16),
            dma((10,)),
            dma((4,)), dma((4,)),
            dma((8,)), dma((8,)),
            dma((8,)), dma((8,)),
            dma((8,)), dma((8,)),
            dma((NZ,)), dma((NZ,)),
            dma((3, 4)), dma((3, 4)),
            dma((4, 4)), dma((4, 4)),
            dma((2, 8)), dma((2, 8)),
            dma((2, 8)), dma((2, 8)),
            dma((2, 4)), dma((2, 4)),
        ],
        compiler_params=pltpu.CompilerParams(
            collective_id=0, has_side_effects=True, vmem_limit_bytes=60 << 20
        ),
    )(hidden_rows, query_proj, key_proj, value_proj, order_pos, post_gain, out_weight)


def solution(mesh):
    placed = (
        P("fsdp", "ctx", None),
        P("fsdp", "ctx", None),
        P("fsdp", "ctx", None),
        P("fsdp", "ctx", None),
        P("fsdp", "ctx"),
        P(),
        P("fsdp", "ctx"),
    )
    return jax.shard_map(
        shards, mesh=mesh, in_specs=placed, out_specs=P("fsdp", "ctx", None), check_vma=False
    )
```

time: 405 us -> 82.4 us (0.20)
  waiting for transfers between devices: 340 us -> 0 us
  Pallas kernels: 0 us -> 79.9 us
  blocking collectives: 20.7 us -> 0 us
  matrix products: 13.2 us -> 0 us
  between operations: 13.2 us -> 0.01 us
  local copies, waits for them, and re-layouts: 9.43 us -> 2.36 us
    all_gather x4 -> x0, waiting for transfers between devices: 324 us -> none  [the longest x1 116 us: shards(): weight_block = lax.all_gather(out_weight, 'fsdp', axis=0, tiled=True)]
    pallas_call x0 -> x1, Pallas kernels: none -> 79.9 us  [shards(): pl.pallas_call(body, name='sublayer', out_shape=jax.ShapeDtypeStruct((1,...]
    all_gather x1 -> x0, blocking collectives: 20.7 us -> none  [shards(): all_positions = lax.all_gather(order_pos, 'ctx', axis=1, tiled=True)[0]]
    all_to_all x1 -> x0, waiting for transfers between devices: 14.6 us -> none  [shards(): lax.all_to_all(projected.astype(jnp.bfloat16), 'ctx', split_axis=0, conca...]
    dot_general x3 -> x0, matrix products: 13.2 us -> none  [the longest x1 5.67 us: shards(): jnp.dot(lax.all_gather(attended, 'ctx', axis=1, tiled=True)[0], weight_bl...]
  transfers between devices with their start and end apart: 5 -> 0, of which waited for: 5 -> 0; matrix products, arithmetic and copies ran while one was open for 4% -> 0% of each run, Pallas kernels for 0% -> 0%
where the time goes in v2:
time: 82.4 us; the launch traced here: 82.3 us
  Pallas kernels  79.9 us (97%)
  local copies, waits for them, and re-layouts  2.36 us (3%)
    pallas_call x1, Pallas kernels, shards(): pl.pallas_call(body, name='sublayer', out_shape=jax.ShapeDtypeStruct((1,...  79.9 us
    unnamed x1, local copies, waits for them, and re-layouts  2.36 us

profile of v2, /device:TPU:1, one launch (start us, length us, event | category | flops | bytes accessed | tf_op | source)
XLA Modules:
  0.0 82.3 jit_solution(2508969795342577353)
XLA Ops:
  0.0 79.9 %sublayer.1 = bf16[1,128,4608]{2,1,0:T(8,128)(2,1)} custom-call(bf16[1,128,4608]{2,1,0:T(8,128)(2,1)} %hid.1, bf16[1,128,2048]{2,1,0:T(8,128)(2,1)} %q.1, bf16[1,128,1024]{2,1,0:T(8,128)(2,1)} %k.1, bf16[1,128,1024]{2,1,0:T(8,128)(2,1)} %v.1, s32[1,128]{1,0:T(1,128)} %pos.1, f32[4608]{0:T(1024)} %gain.1, bf16[32,576]{1,0:T(8,128)(2,1)} %w.1), custom_call_target="tpu_custom_call" | custom-call | tf_op jit(solution)/shard_map/sublayer/pallas_call | solution.py:299
  79.9 2.4 %copy.9 = bf16[1,128,4608]{2,1,0:T(8,128)(2,1)} copy(bf16[1,128,4608]{2,1,0:T(8,128)(2,1)} %sublayer.1) | data formatting | bytes 2359296

commit v3 on v2

--- a/solution.py
+++ b/solution.py
@@ -6,7 +6,6 @@
 from jax.sharding import PartitionSpec as P
 
 D = 4608
-OTHERS = [(0, 1), (1, 0), (1, 1)]
 TB = 128
 HB = 64
 CB = 576
@@ -37,8 +36,11 @@
     def dev_ctx(flip, d):
         return (((xh + flip) % 2) * 4 + (y + d) % 4, fs)
 
-    def dev_x(fh, fl):
-        return (((xh + fh) % 2) * 4 + y, ((xl + fl) % 2) * 32 + fs % 32)
+    def at_x(d):
+        return (xh * 2 + xl + d + 4) % 4
+
+    def dev_x(d):
+        return ((at_x(d) // 2) * 4 + y, (at_x(d) % 2) * 32 + fs % 32)
 
     x_opp = dev_ctx(1, 0)
     sibling = (ctx, fs + 1 - 2 * core)
@@ -60,7 +62,7 @@
         remote(dst, dst, loc.at[6], sem, sibling).wait_recv()
 
     partners = [dev_ctx(f, d) for f in range(2) for d in range(4) if f or d]
-    partners += [dev_x(0, 1), dev_x(1, 1), sibling] + [dev_z(d) for d in AWAY[1:]]
+    partners += [dev_x(1), dev_x(-1), sibling] + [dev_z(d) for d in AWAY[1:]]
     barrier = pltpu.get_barrier_semaphore()
     for dev in partners:
         pl.semaphore_signal(barrier, inc=1, device_id=dev, device_id_type=MESH)
@@ -94,11 +96,12 @@
                 i = f * 4 + d
                 send(pos, pbuf.at[ctx], p_s.at[i], p_r.at[i], dev_ctx(f, d))
 
+    def away(d):
+        return AWAY.index(d if d < 8 else 8) if d > -8 else AWAY.index(8)
+
     own_w = wf.at[xh, xl, core, 0]
-    for r, d in enumerate(AWAY):
-        if r:
-            back = AWAY.index(-d if d < 8 else 8)
-            send(own_w, wf.at[xh, xl, core, back], wz_s.at[r], wz_r.at[back], dev_z(d))
+    for d in (1, -1, 4, -4, 2, -2, 3, -3):
+        send(own_w, wf.at[xh, xl, core, away(-d)], wz_s.at[away(d)], wz_r.at[away(-d)], dev_z(d))
     for d in (1, 3, 2):
         col = pl.multiple_of(((y + d) % 4) * 512, 512)
         send(q.at[0, :, pl.ds(col, 512)], qbuf.at[y], q_s.at[d], q_r.at[d], dev_y(d))
@@ -112,28 +115,45 @@
 
     forward_kv(1)
     forward_kv(3)
+    for side in (1, -1):
+        blk = wf.at[xh, xl, core, away(-4 * side)]
+        arrived(blk, wz_r.at[away(-4 * side)])
+        for e in (4, 3, 2, 1) if side > 0 else (3, 2, 1):
+            r = away(-(4 + e) * side)
+            send(blk, wf.at[xh, xl, core, r], wz_s.at[away((4 + e) * side)], wz_r.at[r], dev_z(e * side))
     forward_kv(2)
 
-    def batch(ref_h, ref_l, c, b):
-        return wf.at[ref_h, ref_l, c, pl.ds(4 * b, 4)]
+    def blocks(d, c, first, n):
+        return wf.at[at_x(d) // 2, at_x(d) % 2, c, pl.ds(first, n)]
 
     def weights_z(b):
         for r in range(max(4 * b, 1), 4 * b + 4):
-            arrived(wf.at[xh, xl, core, r], wz_r.at[r])
-        src = batch(xh, xl, core, b)
-        for i, (fh, fl) in enumerate(OTHERS):
-            send(src, src, wx_s.at[i, b], wx_r.at[i, b], dev_x(fh, fl))
-        send(src, src, sb_s.at[3, b], sb_r.at[3, b], sibling)
+            if AWAY[r] not in (4, -4):
+                arrived(wf.at[xh, xl, core, r], wz_r.at[r])
+        src = blocks(0, core, 4 * b, 4)
+        for side, d in enumerate((1, -1)):
+            send(src, src, wx_s.at[side, b], wx_r.at[side, b], dev_x(d))
+        send(src, src, sb_s.at[0, b], sb_r.at[0, b], sibling)
 
     def weights_x(b):
-        for i, (fh, fl) in enumerate(OTHERS):
-            src = batch((xh + fh) % 2, (xl + fl) % 2, core, b)
-            arrived(src, wx_r.at[i, b])
-            send(src, src, sb_s.at[i, b], sb_r.at[i, b], sibling)
+        for side, d in enumerate((1, -1)):
+            src = blocks(-d, core, 4 * b, 4)
+            arrived(src, wx_r.at[side, b])
+            half = blocks(-d, core, 4 * b + 2 * side, 2)
+            send(half, half, wx_s.at[2 + side, b], wx_r.at[2 + side, b], dev_x(d))
+            send(src, src, sb_s.at[1 + side, b], sb_r.at[1 + side, b], sibling)
+
+    def weights_far(b):
+        for side in range(2):
+            half = blocks(2, core, 4 * b + 2 * side, 2)
+            arrived(half, wx_r.at[2 + side, b])
+            send(half, half, sb_s.at[3 + side, b], sb_r.at[3 + side, b], sibling)
 
     def unfold(b):
-        for i, (fh, fl) in enumerate(OTHERS + [(0, 0)]):
-            arrived(batch((xh + fh) % 2, (xl + fl) % 2, 1 - core, b), sb_r.at[i, b])
+        for i, d in enumerate((0, -1, 1)):
+            arrived(blocks(d, 1 - core, 4 * b, 4), sb_r.at[i, b])
+        for side in range(2):
+            arrived(blocks(2, 1 - core, 4 * b + 2 * side, 2), sb_r.at[3 + side, b])
 
         def piece(i, _):
             l, c = i // 2, i % 2
@@ -207,15 +227,21 @@
 
         return 0
 
-    lax.fori_loop(0, 4, unit, 0)
+    lax.fori_loop(0, 2, unit, 0)
+    weights_x(0)
+    lax.fori_loop(2, 4, unit, 0)
     weights_z(2)
-    weights_x(0)
-    lax.fori_loop(4, 8, unit, 0)
+    lax.fori_loop(4, 6, unit, 0)
+    weights_x(1)
     weights_z(3)
-    weights_x(1)
+    lax.fori_loop(6, 8, unit, 0)
+    weights_far(0)
+    weights_x(2)
+    att_forward(4)
+    weights_far(1)
     unfold(0)
-    att_forward(4)
     att_forward(5)
+    weights_x(3)
 
     far = (y + 2) % 4
 
@@ -265,10 +291,10 @@
         done = pl.ds(p * HB, HB)
         return pltpu.make_async_copy(res.at[done], out.at[0, done], loc.at[8 + p])
 
-    weights_x(2)
+    weights_far(2)
     unfold(1)
     att_forward(6)
-    weights_x(3)
+    weights_far(3)
     unfold(2)
     att_forward(7)
     far_arrived(0)
@@ -323,8 +349,8 @@
             dma((8,)), dma((8,)),
             dma((8,)), dma((8,)),
             dma((NZ,)), dma((NZ,)),
-            dma((3, 4)), dma((3, 4)),
             dma((4, 4)), dma((4, 4)),
+            dma((5, 4)), dma((5, 4)),
             dma((2, 8)), dma((2, 8)),
             dma((2, 8)), dma((2, 8)),
             dma((2, 4)), dma((2, 4)),

time: 82.4 us -> 76.9 us (0.933)
  Pallas kernels: 79.9 us -> 74.3 us
    pallas_call x1, Pallas kernels: 79.9 us -> 74.3 us  [shards(): pl.pallas_call(body, name='sublayer', out_shape=jax.ShapeDtypeStruct((1,...]
where the time goes in v3:
time: 76.9 us; the launch traced here: 76.7 us
  Pallas kernels  74.3 us (97%)
  local copies, waits for them, and re-layouts  2.36 us (3%)
    pallas_call x1, Pallas kernels, shards(): pl.pallas_call(body, name='sublayer', out_shape=jax.ShapeDtypeStruct((1,...  74.3 us
    unnamed x1, local copies, waits for them, and re-layouts  2.36 us

profile of v3, /device:TPU:1, one launch (start us, length us, event | category | flops | bytes accessed | tf_op | source)
XLA Modules:
  0.0 76.7 jit_solution(14031281485087981366)
XLA Ops:
  0.0 74.3 %sublayer.1 = bf16[1,128,4608]{2,1,0:T(8,128)(2,1)} custom-call(bf16[1,128,4608]{2,1,0:T(8,128)(2,1)} %hid.1, bf16[1,128,2048]{2,1,0:T(8,128)(2,1)} %q.1, bf16[1,128,1024]{2,1,0:T(8,128)(2,1)} %k.1, bf16[1,128,1024]{2,1,0:T(8,128)(2,1)} %v.1, s32[1,128]{1,0:T(1,128)} %pos.1, f32[4608]{0:T(1024)} %gain.1, bf16[32,576]{1,0:T(8,128)(2,1)} %w.1), custom_call_target="tpu_custom_call" | custom-call | tf_op jit(solution)/shard_map/sublayer/pallas_call | solution.py:325
  74.4 2.4 %copy.9 = bf16[1,128,4608]{2,1,0:T(8,128)(2,1)} copy(bf16[1,128,4608]{2,1,0:T(8,128)(2,1)} %sublayer.1) | data formatting | bytes 2359296

commit v4 on v3

--- a/solution.py
+++ b/solution.py
@@ -10,6 +10,7 @@
 HB = 64
 CB = 576
 CP = 2 * CB
+NC = CP // 3
 NZ = 16
 INNER = 1.0 / 600.0
 OUTER = 50.0 * 1.4426950408889634
@@ -252,39 +253,41 @@
 
     def project(p):
         def cols(n, _):
-            n = pl.multiple_of(n * 384, 384)
+            col = pl.multiple_of(n * NC, NC)
             r = 0.0
             for src in range(4):
                 a = jnp.concatenate([att[src, p, h] for h in range(4)], axis=1)
-                wb = wg[src // 2, (src % 2) * 8 : (src % 2) * 8 + 8, :, pl.ds(n, 384)].reshape(512, 384)
+                wb = wg[src // 2, (src % 2) * 8 : (src % 2) * 8 + 8, :, pl.ds(col, NC)].reshape(512, NC)
                 r += jnp.dot(a, wb, preferred_element_type=jnp.float32)
-            obuf[p, :, :, pl.ds(n, 384)] = r.astype(jnp.bfloat16).reshape(4, HB, 384)
+            obuf[p, n] = r.astype(jnp.bfloat16).reshape(4, HB, NC)
+            for d in (2, 1, 3):
+                remote(
+                    obuf.at[p, n, (y + d) % 4], rows.at[p, n, y], o_s.at[p, n, d], o_r.at[p, n, d], dev_y(d)
+                ).start()
+            rows[p, n, y] = obuf[p, n, y]
             return 0
 
         lax.fori_loop(0, 3, cols, 0)
-        for d in (2, 1, 3):
-            dst = rows.at[p, y]
-            send(obuf.at[p, (y + d) % 4], dst, o_s.at[p, d], o_r.at[p, d], dev_y(d))
-        rows[p, y] = obuf[p, y]
 
     def norm(p):
         for d in (1, 3, 2):
-            arrived(rows.at[p, (y - d + 4) % 4], o_r.at[p, d])
+            for n in range(3):
+                arrived(rows.at[p, n, (y - d + 4) % 4], o_r.at[p, n, d])
 
         def piece(i, _):
             r = pl.ds(pl.multiple_of(i * 32, 32), 32)
             t = pl.ds(pl.multiple_of(p * HB + i * 32, 32), 32)
             ss = jnp.zeros((32, 1), jnp.float32)
             for c in range(4):
-                x = rows[p, c, r].astype(jnp.float32)
+                x = jnp.concatenate([rows[p, n, c, r] for n in range(3)], axis=1).astype(jnp.float32)
                 ss += jnp.sum(x * x, axis=-1, keepdims=True)
             scale = lax.rsqrt(ss * (1.0 / D) + NORM_EPS)
             for c in range(4):
-                x = rows[p, c, r].astype(jnp.float32) * scale
+                x = jnp.concatenate([rows[p, n, c, r] for n in range(3)], axis=1).astype(jnp.float32) * scale
                 for b in range(2):
                     cols = slice(b * 4 * CB + c * CB, b * 4 * CB + (c + 1) * CB)
-                    n = x[:, b * CB : (b + 1) * CB] * gbuf[:, cols]
-                    res[t, cols] = (hbuf[t, cols].astype(jnp.float32) + n).astype(jnp.bfloat16)
+                    scaled = x[:, b * CB : (b + 1) * CB] * gbuf[:, cols]
+                    res[t, cols] = (hbuf[t, cols].astype(jnp.float32) + scaled).astype(jnp.bfloat16)
             return 0
 
         lax.fori_loop(0, 2, piece, 0)
@@ -311,6 +314,10 @@
 
     for c in sends:
         c.wait_send()
+    for p in range(2):
+        for n in range(3):
+            for d in (1, 2, 3):
+                remote(obuf.at[p, n, 0], obuf.at[p, n, 0], o_s.at[p, n, d], loc.at[6], sibling).wait_send()
     for u in range(8):
         for side in range(2):
             blk = att.at[0, 0, 0]
@@ -338,8 +345,8 @@
             pltpu.VMEM((32, CB), bf16),
             pltpu.VMEM((2, 2, 2, NZ, 16, CP), bf16),
             pltpu.VMEM((2, NZ, 64, CP), bf16),
-            pltpu.VMEM((2, 4, HB, CP), bf16),
-            pltpu.VMEM((2, 4, HB, CP), bf16),
+            pltpu.VMEM((2, 3, 4, HB, NC), bf16),
+            pltpu.VMEM((2, 3, 4, HB, NC), bf16),
             pltpu.VMEM((TB, D), bf16),
             pltpu.VMEM((1, D), f32),
             pltpu.VMEM((TB, D), bf16),
@@ -353,7 +360,7 @@
             dma((5, 4)), dma((5, 4)),
             dma((2, 8)), dma((2, 8)),
             dma((2, 8)), dma((2, 8)),
-            dma((2, 4)), dma((2, 4)),
+            dma((2, 3, 4)), dma((2, 3, 4)),
         ],
         compiler_params=pltpu.CompilerParams(
             collective_id=0, has_side_effects=True, vmem_limit_bytes=60 << 20

time: 76.9 us -> 75.6 us (0.983)
  Pallas kernels: 74.3 us -> 73.1 us
    pallas_call x1, Pallas kernels: 74.3 us -> 73.1 us  [shards(): pl.pallas_call(body, name='sublayer', out_shape=jax.ShapeDtypeStruct((1,...]
where the time goes in v4:
time: 75.6 us; the launch traced here: 75.5 us
  Pallas kernels  73.1 us (97%)
  local copies, waits for them, and re-layouts  2.36 us (3%)
    pallas_call x1, Pallas kernels, shards(): pl.pallas_call(body, name='sublayer', out_shape=jax.ShapeDtypeStruct((1,...  73.1 us
    unnamed x1, local copies, waits for them, and re-layouts  2.36 us

profile of v4, /device:TPU:1, one launch (start us, length us, event | category | flops | bytes accessed | tf_op | source)
XLA Modules:
  0.0 75.5 jit_solution(2837693125855522763)
XLA Ops:
  0.0 73.1 %sublayer.1 = bf16[1,128,4608]{2,1,0:T(8,128)(2,1)} custom-call(bf16[1,128,4608]{2,1,0:T(8,128)(2,1)} %hid.1, bf16[1,128,2048]{2,1,0:T(8,128)(2,1)} %q.1, bf16[1,128,1024]{2,1,0:T(8,128)(2,1)} %k.1, bf16[1,128,1024]{2,1,0:T(8,128)(2,1)} %v.1, s32[1,128]{1,0:T(1,128)} %pos.1, f32[4608]{0:T(1024)} %gain.1, bf16[32,576]{1,0:T(8,128)(2,1)} %w.1), custom_call_target="tpu_custom_call" | custom-call | tf_op jit(solution)/shard_map/sublayer/pallas_call | solution.py:332
  73.1 2.4 %copy.9 = bf16[1,128,4608]{2,1,0:T(8,128)(2,1)} copy(bf16[1,128,4608]{2,1,0:T(8,128)(2,1)} %sublayer.1) | data formatting | bytes 2359296

commit v5 on v4

--- a/solution.py
+++ b/solution.py
@@ -116,13 +116,13 @@
 
     forward_kv(1)
     forward_kv(3)
+    forward_kv(2)
     for side in (1, -1):
         blk = wf.at[xh, xl, core, away(-4 * side)]
         arrived(blk, wz_r.at[away(-4 * side)])
         for e in (4, 3, 2, 1) if side > 0 else (3, 2, 1):
             r = away(-(4 + e) * side)
             send(blk, wf.at[xh, xl, core, r], wz_s.at[away((4 + e) * side)], wz_r.at[r], dev_z(e * side))
-    forward_kv(2)
 
     def blocks(d, c, first, n):
         return wf.at[at_x(d) // 2, at_x(d) % 2, c, pl.ds(first, n)]

time: 75.6 us -> 75.6 us (level)
  no operation moved by 1% of the time
where the time goes in v5:
time: 75.6 us; the launch traced here: 75.5 us
  Pallas kernels  73.1 us (97%)
  local copies, waits for them, and re-layouts  2.36 us (3%)
    pallas_call x1, Pallas kernels, shards(): pl.pallas_call(body, name='sublayer', out_shape=jax.ShapeDtypeStruct((1,...  73.1 us
    unnamed x1, local copies, waits for them, and re-layouts  2.36 us

profile of v5, /device:TPU:1, one launch (start us, length us, event | category | flops | bytes accessed | tf_op | source)
XLA Modules:
  0.0 75.5 jit_solution(10827301529078368846)
XLA Ops:
  0.0 73.1 %sublayer.1 = bf16[1,128,4608]{2,1,0:T(8,128)(2,1)} custom-call(bf16[1,128,4608]{2,1,0:T(8,128)(2,1)} %hid.1, bf16[1,128,2048]{2,1,0:T(8,128)(2,1)} %q.1, bf16[1,128,1024]{2,1,0:T(8,128)(2,1)} %k.1, bf16[1,128,1024]{2,1,0:T(8,128)(2,1)} %v.1, s32[1,128]{1,0:T(1,128)} %pos.1, f32[4608]{0:T(1024)} %gain.1, bf16[32,576]{1,0:T(8,128)(2,1)} %w.1), custom_call_target="tpu_custom_call" | custom-call | tf_op jit(solution)/shard_map/sublayer/pallas_call | solution.py:332
  73.1 2.4 %copy.9 = bf16[1,128,4608]{2,1,0:T(8,128)(2,1)} copy(bf16[1,128,4608]{2,1,0:T(8,128)(2,1)} %sublayer.1) | data formatting | bytes 2359296
